TPU v7x, 32 devices: a whole 2x2x4 slice. The times are simulated.
32 devices in a mesh: groups: 2 (over y), pool: 4 (over z), sub: 2 (over x), chip: 2 (over core).
Axes of the slice: x: 2, y: 2, z: 4, core: 2. Of those that a mesh axis runs over, the one named last changes fastest.
Arguments:
- hidden: bfloat16 [1024, 4096], P(('groups', 'pool', 'sub', 'chip')), parts along dimension 0, may hold values from -6 to 6
- query_weight_matrix: bfloat16 [4096, 4096], P(None, 'pool'), may hold values from -0.09375 to 0.09375
- adapter_down_weight: bfloat16 [64, 64, 4096], P('pool', None, ('sub', 'chip')), may hold values from -0.09375 to 0.09375
- adapter_up_weight: bfloat16 [64, 64, 4096], P('pool', None, ('sub', 'chip')), may hold values from -0.75 to 0.75
- adapter_index_rows: int32 [1024], P(('groups', 'pool', 'sub', 'chip')), parts along dimension 0, may hold values from 0 to 63, as said below
Outputs:
- query: bfloat16 [1024, 4096], P(('groups', 'pool', 'sub', 'chip')), parts along dimension 0
There are 2 independent parts, one for each index of `groups`. A program takes and returns all parts, laid end to end along the dimension named above; an argument that names none is the same for every part. Nothing has to cross between parts.
Inputs may be any that keep to these rules, and one draw needn't show every extreme that they name: A row's owner is adapter_index_rows // 16. In each aligned block of 32 rows (the rows of one device) at most 12 rows have one owner, and in every block some owner has exactly 12 rows.
All inputs are finite; a program needn't handle non-finite values.
Results may differ from a plain program's by a relative error of at most 0.0052.
Values may be sent and summed in bfloat16 or wider, within the bound.
A program may use at most 64 MiB of HBM per device.

v0:
```python
import jax
import jax.numpy as jnp
from jax import lax
from jax.sharding import PartitionSpec as P

ADAPTER_SCALE = 0.5


def owner_rank(owner, count):
    table = (owner[:, None] == jnp.arange(count, dtype=jnp.int32)[None, :]).astype(jnp.int32)
    running = jnp.cumsum(table, axis=0) - table
    return jnp.sum(running * table, axis=1)


def reduced_rank_term(incoming_rows, nearby_adapters, adapter_down_weight, adapter_up_weight):
    adapter_stack, rank_extent, portion_width = adapter_down_weight.shape
    flattened_down = adapter_down_weight.reshape(adapter_stack * rank_extent, portion_width)
    project = lax.dot_general(
        incoming_rows, flattened_down, (((1,), (1,)), ((), ())), preferred_element_type=jnp.float32
    )
    select = nearby_adapters[:, None] == jnp.arange(adapter_stack, dtype=jnp.int32)[None, :]
    partial_low = jnp.sum(
        project.reshape(-1, adapter_stack, rank_extent) * select[:, :, None].astype(jnp.float32),
        axis=1,
    )
    projected_down = lax.psum(partial_low, ("sub", "chip")).astype(jnp.bfloat16)
    spread = (select[:, :, None].astype(jnp.bfloat16) * projected_down[:, None, :]).reshape(
        -1, adapter_stack * rank_extent
    )
    flattened_up = adapter_up_weight.reshape(adapter_stack * rank_extent, portion_width)
    update_term = jnp.dot(spread, flattened_up, preferred_element_type=jnp.float32)
    return (ADAPTER_SCALE * update_term).astype(jnp.bfloat16)


def local(hidden, query_weight_matrix, adapter_down_weight, adapter_up_weight, adapter_index_rows):
    pools = lax.axis_size("pool")
    shards = lax.axis_size(("sub", "chip"))
    shard_index = lax.axis_index(("sub", "chip"))
    row_count, width = hidden.shape
    adapter_stack = adapter_down_weight.shape[0]
    portion_width = adapter_down_weight.shape[2]
    capacity = 2 + row_count // (pools - 1)
    nothing = jnp.zeros((), jnp.bfloat16)
    query_cols = jnp.dot(
        lax.all_gather(hidden, "pool", axis=0, tiled=True),
        query_weight_matrix,
        preferred_element_type=jnp.float32,
    ).astype(jnp.bfloat16)
    block_rows, block_adapters = (
        lax.all_gather(hidden, ("sub", "chip"), axis=0, tiled=True),
        lax.all_gather(adapter_index_rows, ("sub", "chip"), axis=0, tiled=True),
    )
    block_size = shards * row_count
    per_owner = shards * capacity
    combined_output = pools * per_owner
    owner = block_adapters // adapter_stack
    slot = owner * per_owner + owner_rank(owner, pools)
    slot_row = (
        jnp.full((combined_output,), -1, jnp.int32)
        .at[slot]
        .set(jnp.arange(block_size, dtype=jnp.int32))
    )
    filled = slot_row >= 0
    safe_row = jnp.maximum(slot_row, 0)
    my_slice = lax.dynamic_slice_in_dim(block_rows, shard_index * portion_width, portion_width, 1)
    send_rows = jnp.where(filled[:, None], jnp.take(my_slice, safe_row, axis=0), nothing)
    send_adapters = jnp.where(filled, jnp.take(block_adapters % adapter_stack, safe_row), 0)
    received_rows, received_adapters = (
        lax.all_to_all(
            send_rows.reshape(pools, per_owner, portion_width),
            "pool",
            split_axis=0,
            concat_axis=0,
            tiled=True,
        ),
        lax.all_to_all(
            send_adapters.reshape(pools, per_owner), "pool", split_axis=0, concat_axis=0, tiled=True
        ),
    )
    update_term = reduced_rank_term(
        received_rows.reshape(combined_output, portion_width),
        received_adapters.reshape(combined_output),
        adapter_down_weight,
        adapter_up_weight,
    )
    returned = lax.all_to_all(
        update_term.reshape(pools, per_owner, portion_width),
        "pool",
        split_axis=0,
        concat_axis=0,
        tiled=True,
    )
    delta_block = jnp.take(returned.reshape(combined_output, portion_width), slot, axis=0)
    delta_rows = lax.all_to_all(
        delta_block, ("sub", "chip"), split_axis=0, concat_axis=1, tiled=True
    )
    query = lax.all_to_all(query_cols, "pool", split_axis=0, concat_axis=1, tiled=True)
    return (query.astype(jnp.float32) + delta_rows.astype(jnp.float32)).astype(jnp.bfloat16)


def solution(mesh):
    in_specs = (
        P(("groups", "pool", "sub", "chip"), None),
        P(None, "pool"),
        P("pool", None, ("sub", "chip")),
        P("pool", None, ("sub", "chip")),
        P(("groups", "pool", "sub", "chip")),
    )
    out_specs = P(("groups", "pool", "sub", "chip"), None)
    return jax.shard_map(local, mesh=mesh, in_specs=in_specs, out_specs=out_specs, check_vma=False)
```

profile of v0, /device:TPU:0, one launch (start us, length us, event | category | flops | bytes accessed | tf_op | source)
XLA Modules:
  0.0 115.8 jit_solution(494919803565934389)
XLA Ops:
  6.5 0.0 copy-start
  6.5 0.0 all-gather.5.cloned.1.call-start
  6.5 0.7 all-gather.5.cloned.1.call-update
  7.3 1.2 %dynamic-slice = u32[1]{0:T(128)} dynamic-slice(u32[32]{0:T(128)} %constant.102, u32[]{:T(128)S(6)} %add.48), dynamic_slice_sizes={1} | dynamic-slice | bytes 12
  9.2 0.9 dynamic-update-slice
  10.0 6.3 %all-reduce = s32[128]{0:T(128)S(1)} all-reduce(s32[128]{0:T(128)S(1)} %dynamic-update-slice), channel_id=1, replica_groups=mesh['groups'=2,'pool'=4,'sub'=2,'chip'=2] {'sub','chip'}, use_global_device_ids=true, to_apply=%add | all-reduce | flops 128 | bytes 1024
  16.4 0.1 fusion.7
  16.5 0.2 reduce_window_sum.11
  16.7 0.2 select_reduce_fusion
  16.9 1.0 scatter_custom_fusion
  17.9 1.6 %gather_fusion = s32[192]{0:T(256)S(1)} fusion(s32[128]{0:T(128)S(1)} %get-tuple-element.12, s32[1024]{0:T(1024)S(1)} %pad_clamp_fusion.1), kind=kCustom, calls=%fused_computation | custom fusion | bytes 2304 | tf_op jit(solution)/shard_map/jit(_take)/gather | solution.py:67
  19.4 0.7 all_to_all.32
  20.1 4.9 %all-to-all-start.1 = ((s32[4,1,48]{2,1,0:T(1,128)}), s32[4,1,48]{2,1,0:T(1,128)S(1)}, u32[]{:S(2)}, u32[]{:S(2)}) async-start(s32[4,1,48]{2,1,0:T(1,128)} %all_to_all.32), calls=%async_computation.1 | async-start | bytes 4096 | tf_op jit(solution)/shard_map/all_to_all | solution.py:76
  25.0 0.0 all-gather.3.cloned.1.call-start
  25.0 0.7 all-gather.3.cloned.1.call-update
  25.7 0.1 broadcast_in_dim.67
  25.8 0.1 broadcast_in_dim.69
  25.9 2.5 %all-gather.5.cloned.1.call-done = bf16[128,4096]{1,0:T(8,128)(2,1)} async-done(((bf16[32,4096]{1,0:T(8,128)(2,1)}), bf16[128,4096]{1,0:T(8,128)(2,1)}) %all-gather.5.cloned.1.call-update) | async-done | bytes 1048592 | tf_op jit(solution)/shard_map/all_gather | solution.py:50
  28.4 1.0 constant_dynamic-slice_fusion
  29.3 1.0 gather_fusion.1
  30.4 0.9 select_select_fusion
  31.2 0.0 all-to-all-done.1
  31.2 4.6 %all-to-all-start.2 = ((bf16[4,48,1024]{2,1,0:T(8,128)(2,1)}), bf16[4,48,1024]{2,1,0:T(8,128)(2,1)S(1)}, u32[]{:S(2)}, u32[]{:S(2)}) async-start(bf16[4,48,1024]{2,1,0:T(8,128)(2,1)} %select_select_fusion), calls=%async_computation.2 | async-start | bytes 786432 | tf_op jit(solution)/shard_map/all_to_all | solution.py:69
  35.8 0.5 broadcast.96
  36.3 0.7 reduce.3
  37.0 0.1 eq.40
  37.1 20.6 %all-to-all-done.2 = bf16[4,48,1024]{2,1,0:T(8,128)(2,1)S(1)} async-done(((bf16[4,48,1024]{2,1,0:T(8,128)(2,1)}), bf16[4,48,1024]{2,1,0:T(8,128)(2,1)S(1)}, u32[]{:S(2)}, u32[]{:S(2)}) %all-to-all-start.2) | async-done | bytes 393248 | tf_op jit(solution)/shard_map/all_to_all | solution.py:69
  57.7 2.3 %fusion.2 = f32[192,64]{0,1:T(8,128)S(1)} fusion(bf16[192,1024,1]{1,0,2:T(8,128)(2,1)S(1)} %bitcast.27, bf16[16,64,1024]{2,1,0:T(8,128)(2,1)} %param.7, f32[192,16]{0,1:T(8,128)S(1)} %get-tuple-element.11), kind=kOutput, calls=%fused_computation.8 | convolution fusion | flops 403034112 | bytes 2551808 | tf_op jit(solution)/shard_map/dot_general | solution.py:18
  60.1 11.1 %psum.7 = bf16[192,64]{0,1:T(8,128)(2,1)S(1)} all-reduce(f32[192,64]{0,1:T(8,128)S(1)} %fusion.2), channel_id=1, replica_groups=mesh['groups'=2,'pool'=4,'sub'=2,'chip'=2] {'sub','chip'}, use_global_device_ids=true, to_apply=%region_4.5 | all-reduce | flops 12288 | bytes 73728 | tf_op jit(solution)/shard_map/psum | solution.py:26
  71.1 0.0 copy-done
  71.2 1.4 %fusion.1 = bf16[192,1024]{1,0:T(8,128)(2,1)} fusion(bf16[16,64,1024]{2,1,0:T(8,128)(2,1)S(1)} %copy-done, bf16[192,64]{0,1:T(8,128)(2,1)S(1)} %psum.7, bf16[192,16]{0,1:T(8,128)(2,1)S(1)} %get-tuple-element.10), kind=kOutput, calls=%fused_computation.7 | convolution fusion | flops 403243008 | bytes 2521088 | tf_op jit(solution)/shard_map/dot_general | solution.py:31
  72.5 3.5 %all-to-all-start.3 = ((bf16[4,48,1024]{2,1,0:T(8,128)(2,1)}), bf16[4,48,1024]{2,1,0:T(8,128)(2,1)S(1)}, u32[]{:S(2)}, u32[]{:S(2)}) async-start(bf16[4,48,1024]{2,1,0:T(8,128)(2,1)} %bitcast.6), calls=%async_computation.3 | async-start | bytes 786432 | tf_op jit(solution)/shard_map/all_to_all | solution.py:86
  76.0 0.0 all-gather.3.cloned.1.call-done
  76.0 5.7 %convolution_convert_fusion = bf16[128,1024]{1,0:T(8,128)(2,1)} fusion(bf16[128,4096]{1,0:T(8,128)(2,1)} %all-gather.3.cloned.1.call-done, bf16[4096,1024]{1,0:T(8,128)(2,1)} %param.6), kind=kOutput, calls=%fused_computation.9 | convolution fusion | flops 1073872896 | bytes 9699328 | tf_op jit(solution)/shard_map/dot_general | solution.py:44
  81.7 5.7 %all-to-all-done.3 = bf16[4,48,1024]{2,1,0:T(8,128)(2,1)S(1)} async-done(((bf16[4,48,1024]{2,1,0:T(8,128)(2,1)}), bf16[4,48,1024]{2,1,0:T(8,128)(2,1)S(1)}, u32[]{:S(2)}, u32[]{:S(2)}) %all-to-all-start.3) | async-done | bytes 393248 | tf_op jit(solution)/shard_map/all_to_all | solution.py:86
  87.4 3.4 %all-to-all-start = ((bf16[4,32,1024]{2,1,0:T(8,128)(2,1)}), bf16[4,32,1024]{2,1,0:T(8,128)(2,1)S(1)}, u32[]{:S(2)}, u32[]{:S(2)}) async-start(bf16[4,32,1024]{2,1,0:T(8,128)(2,1)} %bitcast), calls=%async_computation | async-start | bytes 524288 | tf_op jit(solution)/shard_map/all_to_all | solution.py:97
  90.8 0.1 broadcast_in_dim.61
  90.9 0.9 gather_fusion.2
  91.7 0.1 broadcast_select_fusion
  91.8 5.7 %all-to-all-done = bf16[4,32,1024]{2,1,0:T(8,128)(2,1)S(1)} async-done(((bf16[4,32,1024]{2,1,0:T(8,128)(2,1)}), bf16[4,32,1024]{2,1,0:T(8,128)(2,1)S(1)}, u32[]{:S(2)}, u32[]{:S(2)}) %all-to-all-start) | async-done | bytes 262176 | tf_op jit(solution)/shard_map/all_to_all | solution.py:97
  97.5 10.6 %all_to_all.42 = bf16[4,32,1024]{2,1,0:T(8,128)(2,1)S(1)} all-to-all(bf16[4,32,1024]{2,1,0:T(8,128)(2,1)S(1)} %broadcast_select_fusion), channel_id=1, replica_groups=mesh['groups'=2,'pool'=4,'sub'=2,'chip'=2] {'sub','chip'}, dimensions={0} | all-to-all | bytes 524288 | tf_op jit(solution)/shard_map/all_to_all | solution.py:94
  108.2 0.1 fusion.4
  108.2 0.7 copy.11
  (9 shorter events, 0.1 us)
Async XLA Ops:
  6.5 64.6 %copy-start = (bf16[16,64,1024]{2,1,0:T(8,128)(2,1)S(1)}, bf16[16,64,1024]{2,1,0:T(8,128)(2,1)}, u32[]{:S(2)}) copy-start(bf16[16,64,1024]{2,1,0:T(8,128)(2,1)} %param.8) | copy-start | bytes 6291460
  6.5 21.8 %all-gather.5.cloned.1.call-start = ((), (), s32[]{:S(2)}) async-start(), calls=%async_computation.6 | async-start | bytes 1310720 | tf_op jit(solution)/shard_map/all_gather | solution.py:50
  20.1 11.1 %all-to-all-start.1 = ((s32[4,1,48]{2,1,0:T(1,128)}), s32[4,1,48]{2,1,0:T(1,128)S(1)}, u32[]{:S(2)}, u32[]{:S(2)}) async-start(s32[4,1,48]{2,1,0:T(1,128)} %all_to_all.32), calls=%async_computation.1 | async-start | bytes 4096 | tf_op jit(solution)/shard_map/all_to_all | solution.py:76
  25.0 51.0 %all-gather.3.cloned.1.call-start = ((), (), s32[]{:S(2)}) async-start(), calls=%async_computation.5 | async-start | bytes 1310720 | tf_op jit(solution)/shard_map/all_gather | solution.py:45
  31.2 26.5 %all-to-all-start.2 = ((bf16[4,48,1024]{2,1,0:T(8,128)(2,1)}), bf16[4,48,1024]{2,1,0:T(8,128)(2,1)S(1)}, u32[]{:S(2)}, u32[]{:S(2)}) async-start(bf16[4,48,1024]{2,1,0:T(8,128)(2,1)} %select_select_fusion), calls=%async_computation.2 | async-start | bytes 786432 | tf_op jit(solution)/shard_map/all_to_all | solution.py:69
  72.5 14.8 %all-to-all-start.3 = ((bf16[4,48,1024]{2,1,0:T(8,128)(2,1)}), bf16[4,48,1024]{2,1,0:T(8,128)(2,1)S(1)}, u32[]{:S(2)}, u32[]{:S(2)}) async-start(bf16[4,48,1024]{2,1,0:T(8,128)(2,1)} %bitcast.6), calls=%async_computation.3 | async-start | bytes 786432 | tf_op jit(solution)/shard_map/all_to_all | solution.py:86
  87.4 10.2 %all-to-all-start = ((bf16[4,32,1024]{2,1,0:T(8,128)(2,1)}), bf16[4,32,1024]{2,1,0:T(8,128)(2,1)S(1)}, u32[]{:S(2)}, u32[]{:S(2)}) async-start(bf16[4,32,1024]{2,1,0:T(8,128)(2,1)} %bitcast), calls=%async_computation | async-start | bytes 524288 | tf_op jit(solution)/shard_map/all_to_all | solution.py:97
Sparse Core Ops, SparseCore 0:
  8.9 19.4 all-gather.4
  29.9 35.1 all-gather.2
where the time goes:
time: 116 us
  waiting for transfers between devices  35.9 us (31%)
  blocking collectives  28.1 us (24%)
  starting transfers between devices  16.3 us (14%)
  between operations  14.2 us (12%)
  local copies, waits for them, and re-layouts  9.72 us (8%)
  matrix products  9.37 us (8%)
  other arithmetic  2.18 us (2%)
    all_to_all x1, waiting for transfers between devices, local(): lax.all_to_all(send_rows.reshape(pools, per_owner, portion_width), 'pool'...  20.6 us
    psum x1, blocking collectives, reduced_rank_term(): projected_down = lax.psum(partial_low, ('sub', 'chip')).astype(jnp.bfloat16)  11.1 us
    all_to_all x1, blocking collectives, local(): lax.all_to_all(delta_block, ('sub', 'chip'), split_axis=0, concat_axis=1,...  10.6 us
    unnamed x1, blocking collectives  6.35 us
    all_to_all x1, waiting for transfers between devices, local(): lax.all_to_all(query_cols, 'pool', split_axis=0, concat_axis=1, tiled=True)  5.69 us
    dot_general x1, matrix products, local(): jnp.dot(lax.all_gather(hidden, 'pool', axis=0, tiled=True), query_weight_...  5.68 us
    all_to_all x1, waiting for transfers between devices, local(): lax.all_to_all(update_term.reshape(pools, per_owner, portion_width), 'poo...  5.67 us
    all_to_all x1, starting transfers between devices, local(): lax.all_to_all(send_adapters.reshape(pools, per_owner), 'pool', split_axi...  4.87 us
  transfers between devices with their start and end apart: 6, of which 4 were waited for; matrix products, arithmetic and copies ran while one was open for 17% of the time, Pallas kernels for 0%

commit v1 on v0

--- a/solution.py
+++ b/solution.py
@@ -4,6 +4,28 @@
 from jax.sharding import PartitionSpec as P
 
 ADAPTER_SCALE = 0.5
+
+
+def laid_out(blocks, dim):
+    lengths = list(blocks.shape[1:])
+    lengths[dim] *= blocks.shape[0]
+    return jnp.moveaxis(blocks, 0, dim).reshape(lengths)
+
+
+def gather_around(x, axis, dim):
+    size = lax.axis_size(axis)
+    pairs = [(i, (i + 1) % size) for i in range(size)]
+    back = [(b, a) for a, b in pairs]
+    lower, upper = ([], [])
+    for turn in range(size - 1):
+        if turn % 2 == 0:
+            lower.append(lax.ppermute(lower[-1] if lower else x, axis, pairs))
+        else:
+            upper.append(lax.ppermute(upper[-1] if upper else x, axis, back))
+    blocks = jnp.stack([*lower[::-1], x, *upper])
+    shift = lax.axis_index(axis) - len(lower)
+    blocks = blocks[(jnp.arange(size) - shift) % size]
+    return laid_out(blocks, dim)
 
 
 def owner_rank(owner, count):
@@ -47,7 +69,7 @@
         preferred_element_type=jnp.float32,
     ).astype(jnp.bfloat16)
     block_rows, block_adapters = (
-        lax.all_gather(hidden, ("sub", "chip"), axis=0, tiled=True),
+        gather_around(hidden, ("sub", "chip"), 0),
         lax.all_gather(adapter_index_rows, ("sub", "chip"), axis=0, tiled=True),
     )
     block_size = shards * row_count

time: 116 us -> 111 us (0.957)
  waiting for transfers between devices: 35.9 us -> 23.4 us
  starting transfers between devices: 16.3 us -> 19.3 us
  local copies, waits for them, and re-layouts: 9.72 us -> 12 us
  other arithmetic: 2.18 us -> 4.15 us
    all_to_all x1, waiting for transfers between devices: 20.6 us -> 10.4 us  [local(): lax.all_to_all(send_rows.reshape(pools, per_owner, portion_width), 'pool'...]
    all_to_all x1, waiting for transfers between devices: 5.67 us -> 11.3 us  [local(): lax.all_to_all(update_term.reshape(pools, per_owner, portion_width), 'poo...]
    all_to_all x1, waiting for transfers between devices: 5.69 us -> 0.99 us  [local(): lax.all_to_all(delta_block, ('sub', 'chip'), split_axis=0, concat_axis=1,...]
    all_gather x1 -> x0, waiting for transfers between devices: 2.49 us -> none  [local(): lax.all_gather(hidden, ('sub', 'chip'), axis=0, tiled=True)]
    ppermute x0 -> x3, starting transfers between devices: none -> 2.44 us  [the longest x1 1.93 us: gather_around(): upper.append(lax.ppermute(upper[-1] if upper else x, axis, back))]
    gather x0 -> x1, local copies, waits for them, and re-layouts: none -> 1.59 us  [gather_around(): blocks = blocks[(jnp.arange(size) - shift) % size]]
    another operation x0 -> x1, other arithmetic: none -> 1.24 us  [gather_around(): blocks = jnp.stack([*lower[::-1], x, *upper])]
    unnamed x5 -> x9, local copies, waits for them, and re-layouts: 2.11 us -> 2.84 us
  transfers between devices with their start and end apart: 6 -> 8, of which waited for: 4 -> 3; matrix products, arithmetic and copies ran while one was open for 17% -> 21% of each run, Pallas kernels for 0% -> 0%
where the time goes in v1:
time: 111 us; the launch traced here: 110 us
  blocking collectives  28.6 us (26%)
  waiting for transfers between devices  23.4 us (21%)
  starting transfers between devices  19.3 us (17%)
  between operations  14.2 us (13%)
  local copies, waits for them, and re-layouts  12 us (11%)
  matrix products  8.66 us (8%)
  other arithmetic  4.15 us (4%)
    psum x1, blocking collectives, reduced_rank_term(): projected_down = lax.psum(partial_low, ('sub', 'chip')).astype(jnp.bfloat16)  11.6 us
    all_to_all x1, blocking collectives, local(): lax.all_to_all(query_cols, 'pool', split_axis=0, concat_axis=1, tiled=True)  11.3 us
    all_to_all x1, waiting for transfers between devices, local(): lax.all_to_all(update_term.reshape(pools, per_owner, portion_width), 'poo...  11.3 us
    all_to_all x1, waiting for transfers between devices, local(): lax.all_to_all(send_rows.reshape(pools, per_owner, portion_width), 'pool'...  10.4 us
    unnamed x1, blocking collectives  5.72 us
    all_to_all x1, starting transfers between devices, local(): lax.all_to_all(send_rows.reshape(pools, per_owner, portion_width), 'pool'...  5.09 us
    dot_general x1, matrix products, local(): jnp.dot(lax.all_gather(hidden, 'pool', axis=0, tiled=True), query_weight_...  4.97 us
    all_to_all x1, starting transfers between devices, local(): lax.all_to_all(send_adapters.reshape(pools, per_owner), 'pool', split_axi...  4.87 us
  transfers between devices with their start and end apart: 8, of which 3 were waited for; matrix products, arithmetic and copies ran while one was open for 21% of the time, Pallas kernels for 0%

profile of v1, /device:TPU:0, one launch (start us, length us, event | category | flops | bytes accessed | tf_op | source)
XLA Modules:
  0.0 110.4 jit_solution(17005163441212519031)
XLA Ops:
  6.5 0.5 collective-permute-start
  7.0 1.9 %collective-permute-start.2 = (bf16[32,4096]{1,0:T(8,128)(2,1)}, bf16[32,4096]{1,0:T(8,128)(2,1)S(1)}, u32[]{:S(2)}, u32[]{:S(2)}) collective-permute-start(bf16[32,4096]{1,0:T(8,128)(2,1)} %param.5), channel_id=1, source_target_pairs={{1,0},{2,1},{3,2},{0,3},{5,4},{6,5},{7,6},{4,7},{9,8},{10,9},{11,1... | collective-permute-start | bytes 786440 | tf_op jit(solution)/shard_map/ppermute | solution.py:24
  8.9 1.2 %dynamic-slice = u32[1]{0:T(128)} dynamic-slice(u32[32]{0:T(128)} %constant.119, u32[]{:T(128)S(6)} %add.75), dynamic_slice_sizes={1} | dynamic-slice | bytes 12
  10.8 0.9 dynamic-update-slice
  11.7 5.7 %all-reduce = s32[128]{0:T(128)S(1)} all-reduce(s32[128]{0:T(128)S(1)} %dynamic-update-slice), channel_id=1, replica_groups=mesh['groups'=2,'pool'=4,'sub'=2,'chip'=2] {'sub','chip'}, use_global_device_ids=true, to_apply=%add | all-reduce | flops 128 | bytes 1024
  17.4 0.1 fusion.7
  17.5 0.2 reduce_window_sum.11
  17.7 0.2 select_reduce_fusion
  17.9 1.0 scatter_custom_fusion
  18.9 1.6 %gather_fusion = s32[192]{0:T(256)S(1)} fusion(s32[128]{0:T(128)S(1)} %get-tuple-element.12, s32[1024]{0:T(1024)S(1)} %pad_clamp_fusion.2), kind=kCustom, calls=%fused_computation | custom fusion | bytes 2304 | tf_op jit(solution)/shard_map/jit(_take)/gather | solution.py:89
  20.4 0.0 collective-permute-done
  20.4 0.1 collective-permute-start.1
  20.5 0.6 all_to_all.32
  21.2 4.9 %all-to-all-start.1 = ((s32[4,1,48]{2,1,0:T(1,128)}), s32[4,1,48]{2,1,0:T(1,128)S(1)}, u32[]{:S(2)}, u32[]{:S(2)}) async-start(s32[4,1,48]{2,1,0:T(1,128)} %all_to_all.32), calls=%async_computation.1 | async-start | bytes 4096 | tf_op jit(solution)/shard_map/all_to_all | solution.py:98
  26.0 0.1 broadcast_in_dim.68
  26.1 0.1 broadcast_in_dim.70
  26.2 0.0 collective-permute-done.2
  26.3 0.0 copy-start.1
  26.3 0.0 collective-permute-done.1
  26.3 0.7 copy-done.1
  27.0 0.1 copy-done.2
  27.0 1.2 %pad_maximum_fusion = bf16[4,32,4096]{2,1,0:T(8,128)(2,1)S(1)} fusion(bf16[1,32,4096]{2,1,0:T(8,128)(2,1)} %bitcast.39, bf16[1,32,4096]{2,1,0:T(8,128)(2,1)} %bitcast.36, bf16[1,32,4096]{2,1,0:T(8,128)(2,1)S(1)} %bitcast.38, bf16[1,32,4096]{2,1,0:T(8,128)(2,1)} %bitcast.40), kind=kLoop, calls=%fused_computation.11 | loop fusion | flops 1572864 | bytes 2097152 | tf_op jit(solution)/shard_map/stack | solution.py:25
  28.3 1.6 %gather_fusion.1 = bf16[4,32,4096]{2,1,0:T(8,128)(2,1)} fusion(bf16[4,32,4096]{2,1,0:T(8,128)(2,1)S(1)} %pad_maximum_fusion, s32[1024]{0:T(1024)S(1)} %pad_clamp_fusion.1), kind=kCustom, calls=%fused_computation.1 | custom fusion | bytes 2097168 | tf_op jit(solution)/shard_map/gather | solution.py:27
  29.9 1.0 constant_dynamic-slice_fusion
  30.8 1.0 gather_fusion.2
  31.8 0.9 select_select_fusion
  32.7 0.0 all-to-all-done.1
  32.7 5.1 %all-to-all-start.2 = ((bf16[4,48,1024]{2,1,0:T(8,128)(2,1)}), bf16[4,48,1024]{2,1,0:T(8,128)(2,1)S(1)}, u32[]{:S(2)}, u32[]{:S(2)}) async-start(bf16[4,48,1024]{2,1,0:T(8,128)(2,1)} %select_select_fusion), calls=%async_computation.2 | async-start | bytes 786432 | tf_op jit(solution)/shard_map/all_to_all | solution.py:91
  37.8 0.7 all-gather.2.cloned.1.call-update
  38.5 0.5 broadcast.165
  39.1 0.7 reduce.3
  39.7 0.1 eq.42
  39.8 10.4 %all-to-all-done.2 = bf16[4,48,1024]{2,1,0:T(8,128)(2,1)S(1)} async-done(((bf16[4,48,1024]{2,1,0:T(8,128)(2,1)}), bf16[4,48,1024]{2,1,0:T(8,128)(2,1)S(1)}, u32[]{:S(2)}, u32[]{:S(2)}) %all-to-all-start.2) | async-done | bytes 393248 | tf_op jit(solution)/shard_map/all_to_all | solution.py:91
  50.2 2.3 %fusion.2 = f32[192,64]{0,1:T(8,128)S(1)} fusion(bf16[192,1024,1]{1,0,2:T(8,128)(2,1)S(1)} %bitcast.37, bf16[16,64,1024]{2,1,0:T(8,128)(2,1)} %param.7, f32[192,16]{0,1:T(8,128)S(1)} %get-tuple-element.11), kind=kOutput, calls=%fused_computation.9 | convolution fusion | flops 403034112 | bytes 2551808 | tf_op jit(solution)/shard_map/dot_general | solution.py:40
  52.5 11.6 %psum.7 = bf16[192,64]{0,1:T(8,128)(2,1)S(1)} all-reduce(f32[192,64]{0,1:T(8,128)S(1)} %fusion.2), channel_id=1, replica_groups=mesh['groups'=2,'pool'=4,'sub'=2,'chip'=2] {'sub','chip'}, use_global_device_ids=true, to_apply=%region_4.5 | all-reduce | flops 12288 | bytes 73728 | tf_op jit(solution)/shard_map/psum | solution.py:48
  64.1 1.4 %fusion.1 = bf16[192,1024]{1,0:T(8,128)(2,1)} fusion(bf16[16,64,1024]{2,1,0:T(8,128)(2,1)S(1)} %copy-done, bf16[192,64]{0,1:T(8,128)(2,1)S(1)} %psum.7, bf16[192,16]{0,1:T(8,128)(2,1)S(1)} %get-tuple-element.10), kind=kOutput, calls=%fused_computation.8 | convolution fusion | flops 403243008 | bytes 2521088 | tf_op jit(solution)/shard_map/dot_general | solution.py:53
  65.5 3.5 %all-to-all-start.3 = ((bf16[4,48,1024]{2,1,0:T(8,128)(2,1)}), bf16[4,48,1024]{2,1,0:T(8,128)(2,1)S(1)}, u32[]{:S(2)}, u32[]{:S(2)}) async-start(bf16[4,48,1024]{2,1,0:T(8,128)(2,1)} %bitcast.12), calls=%async_computation.3 | async-start | bytes 786432 | tf_op jit(solution)/shard_map/all_to_all | solution.py:108
  69.0 0.1 broadcast_in_dim.62
  69.1 11.3 %all-to-all-done.3 = bf16[4,48,1024]{2,1,0:T(8,128)(2,1)S(1)} async-done(((bf16[4,48,1024]{2,1,0:T(8,128)(2,1)}), bf16[4,48,1024]{2,1,0:T(8,128)(2,1)S(1)}, u32[]{:S(2)}, u32[]{:S(2)}) %all-to-all-start.3) | async-done | bytes 393248 | tf_op jit(solution)/shard_map/all_to_all | solution.py:108
  80.3 0.9 gather_fusion.3
  81.2 0.8 broadcast_select_fusion
  82.0 3.4 %all-to-all-start.4 = ((bf16[4,32,1024]{2,1,0:T(8,128)(2,1)}), bf16[4,32,1024]{2,1,0:T(8,128)(2,1)S(1)}, u32[]{:S(2)}, u32[]{:S(2)}) async-start(bf16[4,32,1024]{2,1,0:T(8,128)(2,1)} %broadcast_select_fusion), calls=%async_computation.4 | async-start | bytes 524288 | tf_op jit(solution)/shard_map/all_to_all | solution.py:116
  85.4 0.0 all-gather.2.cloned.1.call-done
  85.4 5.0 %convolution_convert_fusion = bf16[128,1024]{1,0:T(8,128)(2,1)S(1)} fusion(bf16[128,4096]{1,0:T(8,128)(2,1)} %all-gather.2.cloned.1.call-done, bf16[4096,1024]{1,0:T(8,128)(2,1)} %param.6), kind=kOutput, calls=%fused_computation.10 | convolution fusion | flops 1073872896 | bytes 9699328 | tf_op jit(solution)/shard_map/dot_general | solution.py:66
  90.4 1.0 all-to-all-done.4
  91.4 11.3 %all_to_all.42 = bf16[4,32,1024]{2,1,0:T(8,128)(2,1)S(1)} all-to-all(bf16[4,32,1024]{2,1,0:T(8,128)(2,1)S(1)} %bitcast.34), channel_id=1, replica_groups=mesh['groups'=2,'pool'=4,'sub'=2,'chip'=2] {'pool'}, dimensions={0} | all-to-all | bytes 524288 | tf_op jit(solution)/shard_map/all_to_all | solution.py:119
  102.8 0.1 fusion.4
  102.8 0.7 copy.11
  (15 shorter events, 0.1 us)
Async XLA Ops:
  6.5 57.6 %copy-start = (bf16[16,64,1024]{2,1,0:T(8,128)(2,1)S(1)}, bf16[16,64,1024]{2,1,0:T(8,128)(2,1)}, u32[]{:S(2)}) copy-start(bf16[16,64,1024]{2,1,0:T(8,128)(2,1)} %param.8) | copy-start | bytes 6291460
  6.5 13.9 %collective-permute-start = (bf16[32,4096]{1,0:T(8,128)(2,1)}, bf16[32,4096]{1,0:T(8,128)(2,1)S(1)}, u32[]{:S(2)}, u32[]{:S(2)}) collective-permute-start(bf16[32,4096]{1,0:T(8,128)(2,1)} %param.5), channel_id=1, source_target_pairs={{0,1},{1,2},{2,3},{3,0},{4,5},{5,6},{6,7},{7,4},{8,9},{9,10},{10,1... | collective-permute-start | bytes 786440 | tf_op jit(solution)/shard_map/ppermute | solution.py:22
  7.0 19.3 %collective-permute-start.2 = (bf16[32,4096]{1,0:T(8,128)(2,1)}, bf16[32,4096]{1,0:T(8,128)(2,1)S(1)}, u32[]{:S(2)}, u32[]{:S(2)}) collective-permute-start(bf16[32,4096]{1,0:T(8,128)(2,1)} %param.5), channel_id=1, source_target_pairs={{1,0},{2,1},{3,2},{0,3},{5,4},{6,5},{7,6},{4,7},{9,8},{10,9},{11,1... | collective-permute-start | bytes 786440 | tf_op jit(solution)/shard_map/ppermute | solution.py:24
  20.4 5.8 %collective-permute-start.1 = (bf16[32,4096]{1,0:T(8,128)(2,1)S(1)}, bf16[32,4096]{1,0:T(8,128)(2,1)S(1)}, u32[]{:S(2)}, u32[]{:S(2)}) collective-permute-start(bf16[32,4096]{1,0:T(8,128)(2,1)S(1)} %collective-permute-done), channel_id=1, source_target_pairs={{0,1},{1,2},{2,3},{3,0},{4,5},{5,6},{6,7},{7,4},{8,9},{9,10},{10,1... | collective-permute-start | bytes 786440 | tf_op jit(solution)/shard_map/ppermute | solution.py:22
  21.2 11.6 %all-to-all-start.1 = ((s32[4,1,48]{2,1,0:T(1,128)}), s32[4,1,48]{2,1,0:T(1,128)S(1)}, u32[]{:S(2)}, u32[]{:S(2)}) async-start(s32[4,1,48]{2,1,0:T(1,128)} %all_to_all.32), calls=%async_computation.1 | async-start | bytes 4096 | tf_op jit(solution)/shard_map/all_to_all | solution.py:98
  26.3 0.7 copy-start.1
  26.3 0.7 copy-start.2
  32.7 17.5 %all-to-all-start.2 = ((bf16[4,48,1024]{2,1,0:T(8,128)(2,1)}), bf16[4,48,1024]{2,1,0:T(8,128)(2,1)S(1)}, u32[]{:S(2)}, u32[]{:S(2)}) async-start(bf16[4,48,1024]{2,1,0:T(8,128)(2,1)} %select_select_fusion), calls=%async_computation.2 | async-start | bytes 786432 | tf_op jit(solution)/shard_map/all_to_all | solution.py:91
  37.8 47.6 %all-gather.2.cloned.1.call-start = ((), (), s32[]{:S(2)}) async-start(), calls=%async_computation.5 | async-start | bytes 1310720 | tf_op jit(solution)/shard_map/all_gather | solution.py:67
  65.5 14.9 %all-to-all-start.3 = ((bf16[4,48,1024]{2,1,0:T(8,128)(2,1)}), bf16[4,48,1024]{2,1,0:T(8,128)(2,1)S(1)}, u32[]{:S(2)}, u32[]{:S(2)}) async-start(bf16[4,48,1024]{2,1,0:T(8,128)(2,1)} %bitcast.12), calls=%async_computation.3 | async-start | bytes 786432 | tf_op jit(solution)/shard_map/all_to_all | solution.py:108
  82.0 9.4 %all-to-all-start.4 = ((bf16[4,32,1024]{2,1,0:T(8,128)(2,1)}), bf16[4,32,1024]{2,1,0:T(8,128)(2,1)S(1)}, u32[]{:S(2)}, u32[]{:S(2)}) async-start(bf16[4,32,1024]{2,1,0:T(8,128)(2,1)} %broadcast_select_fusion), calls=%async_computation.4 | async-start | bytes 524288 | tf_op jit(solution)/shard_map/all_to_all | solution.py:116
Sparse Core Ops, SparseCore 0:
  40.2 28.9 all-gather.1
